TPU v7x, 32 devices: a whole 2x2x4 slice. The times are simulated.
32 devices in a mesh: tm: 4 (over y, x), tmpl: 8 (over z, core).
Axes of the slice: x: 2, y: 2, z: 4, core: 2. Of those that a mesh axis runs over, the one named last changes fastest.
Arguments:
- strain: float32 [3, 2048], P(None, 'tm'), may hold values from -21 to 21
- gate_lengths: int32 [16], replicated, may hold values from 1 to 256, 2048 in all
- filters: bfloat16 [8, 1024, 512], P('tmpl'), may hold values from -0.1875 to 0.1875
- mixing: bfloat16 [512, 2, 8192], P(None, None, 'tmpl'), may hold values from -2 to 2
Outputs:
- marginal: float32 [2048], P('tm')
Inputs may be any that keep to these rules, and one draw needn't show every extreme that they name: `gate_lengths`: the 16 lengths sum to 2048; the largest is exactly 256.
All inputs are finite; a program needn't handle non-finite values.
Results may differ from a plain program's by a relative error of at most 0.0019.
Values may be sent and summed in bfloat16 or wider, within the bound.
A program may use at most 64 MiB of HBM per device.

v0:
```python
import math

import jax
import jax.numpy as jnp
from jax import lax
from jax.sharding import PartitionSpec as P


def shifted(block, axis, distance):
    devices = range(lax.axis_size(axis))
    route = [(i - distance, i) for i in devices if i - distance in devices]
    return lax.ppermute(block, axis, route)


def apply_gates(strain, gate_lengths, positions):
    bounds = jnp.cumsum(gate_lengths)
    passed = jnp.sum((bounds[None, :] <= positions[:, None]).astype(jnp.int32), axis=1)
    keep = (passed % 2 == 0).astype(jnp.float32)
    return strain * keep[None, :]


def sliding_windows(extended, segment_length, tap_count):
    det_count, span = extended.shape
    repeated = jnp.tile(extended, (1, segment_length + 1))
    skewed = repeated[:, : segment_length * (span + 1)].reshape(det_count, segment_length, span + 1)
    return skewed[:, :, :tap_count]


def shards(strain, gate_lengths, filters, mixing):
    det_count, segment_length = strain.shape
    tap_count = filters.shape[1]
    basis_width = filters.shape[2]
    template_count = mixing.shape[2]
    positions = lax.axis_index("tm") * segment_length + jnp.arange(segment_length, dtype=jnp.int32)
    gated = apply_gates(strain, gate_lengths, positions).astype(jnp.bfloat16)
    rim_count = (tap_count + segment_length - 2) // segment_length
    needed = segment_length + tap_count - 1
    pieces = [gated]
    moving = gated
    for hop_index in range(rim_count):
        moving = shifted(moving, "tm", 1)
        pieces.insert(0, moving)
    extended = jnp.concatenate(pieces, axis=1)[:, -needed:]
    windows = sliding_windows(extended, segment_length, tap_count)
    basis = jnp.einsum("dtk,kb->dtb", windows, filters[0], preferred_element_type=jnp.float32)
    flat = basis.astype(jnp.bfloat16).reshape(-1, basis_width)
    signal = jnp.dot(
        flat, mixing.reshape(basis_width, 2 * template_count), preferred_element_type=jnp.float32
    )
    signal = signal.reshape(det_count, segment_length, 2, template_count)
    scores = 0.5 * jnp.sum(signal * signal, axis=(0, 2))
    local_peak = jnp.max(scores, axis=1)
    local_total = jnp.sum(jnp.exp(scores - local_peak[:, None]), axis=1)
    overall = lax.pmax(local_peak, "tmpl")
    total = lax.psum(local_total * jnp.exp(local_peak - overall), "tmpl")
    return overall + jnp.log(total) - math.log(template_count * lax.axis_size("tmpl"))


def solution(mesh):
    in_specs = (P(None, "tm"), P(), P("tmpl", None, None), P(None, None, "tmpl"))
    out_specs = P("tm")
    return jax.shard_map(shards, mesh=mesh, in_specs=in_specs, out_specs=out_specs, check_vma=False)
```

profile of v0, /device:TPU:0, one launch (start us, length us, event | category | flops | bytes accessed | tf_op | source)
XLA Modules:
  0.0 84.3 jit_solution(10942066780382975380)
XLA Ops:
  0.0 0.0 copy-start
  0.0 0.8 copy.9
  0.9 0.1 reduce
  1.0 0.1 convert_reduce_fusion
  1.1 0.7 multiply_convert_fusion
  1.8 4.8 %collective-permute-start = (bf16[3,512]{1,0:T(4,128)(2,1)S(1)}, bf16[3,512]{1,0:T(4,128)(2,1)S(1)}, u32[]{:S(2)}, u32[]{:S(2)}) collective-permute-start(bf16[3,512]{1,0:T(4,128)(2,1)S(1)} %multiply_convert_fusion), channel_id=1, source_target_pairs={{0,8},{8,16},{16,24},{1,9},{9,17},{17,25},{2,10},{10,18},{18,26},{... | collective-permute-start | bytes 9224 | tf_op jit(solution)/shard_map/ppermute | solution.py:12
  6.6 1.3 %collective-permute-done = bf16[3,512]{1,0:T(4,128)(2,1)S(1)} collective-permute-done((bf16[3,512]{1,0:T(4,128)(2,1)S(1)}, bf16[3,512]{1,0:T(4,128)(2,1)S(1)}, u32[]{:S(2)}, u32[]{:S(2)}) %collective-permute-start) | collective-permute-done | bytes 3104 | tf_op jit(solution)/shard_map/ppermute | solution.py:12
  7.9 4.2 %collective-permute-start.1 = (bf16[3,512]{1,0:T(4,128)(2,1)S(1)}, bf16[3,512]{1,0:T(4,128)(2,1)S(1)}, u32[]{:S(2)}, u32[]{:S(2)}) collective-permute-start(bf16[3,512]{1,0:T(4,128)(2,1)S(1)} %collective-permute-done), channel_id=1, source_target_pairs={{0,8},{8,16},{16,24},{1,9},{9,17},{17,25},{2,10},{10,18},{18,26},{... | collective-permute-start | bytes 9224 | tf_op jit(solution)/shard_map/ppermute | solution.py:12
  12.1 2.2 %copy.13 = bf16[64,8,2,1024]{3,1,2,0:T(8,128)(2,1)S(1)} copy(bf16[64,8,2,1024]{3,2,1,0:T(2,128)(2,1)} %bitcast.29) | data formatting | bytes 4194304
  14.3 2.5 %copy.10 = bf16[2048,512]{1,0:T(8,128)(2,1)} copy(bf16[2048,512]{0,1:T(8,128)(2,1)S(1)} %bitcast.27) | data formatting | bytes 4194304 | tf_op jit(solution)/shard_map/dot_general | solution.py:47
  16.8 0.0 collective-permute-done.1
  16.8 0.1 pad_maximum_fusion
  16.9 2.6 %tile.4 = bf16[3,513,1535]{2,1,0:T(8,128)(2,1)} broadcast(bf16[3,1535]{1,0:T(4,128)(2,1)S(1)} %pad_maximum_fusion), dimensions={0,2} | broadcast | bytes 4733940 | tf_op jit(solution)/shard_map/tile | solution.py:24
  19.5 13.1 %reshape.67 = bf16[2362365]{0:T(1024)(128)(2,1)} reshape(bf16[3,513,1535]{2,1,0:T(8,128)(2,1)} %tile.4) | data formatting | bytes 9449460
  32.6 7.8 %tile.10 = bf16[3,787455]{1,0:T(4,128)(2,1)} reshape(bf16[2362365]{0:T(1024)(128)(2,1)} %reshape.67) | data formatting | bytes 9449460 | tf_op jit(solution)/shard_map/tile | solution.py:24
  40.5 2.8 %slice-done = bf16[3,786432]{1,0:T(4,128)(2,1)S(1)} async-done(((bf16[3,787455]{1,0:T(4,128)(2,1)}), bf16[3,786432]{1,0:T(4,128)(2,1)S(1)}, s32[]{:S(2)}) %slice-start) | async-done | bytes 4718616 | tf_op jit(solution)/shard_map/slice | solution.py:25
  43.3 3.4 %copy.15 = bf16[1,3,512,1536]{3,2,1,0:T(8,128)(2,1)} copy(bf16[1,3,512,1536]{3,1,2,0:T(4,128)(2,1)S(1)} %bitcast.26) | data formatting | bytes 9437184
  46.7 0.0 copy-done
  46.7 7.5 %multiply_reduce_fusion = f32[512,1024]{1,0:T(8,128)S(1)} fusion(bf16[2,1024,512,1]{2,1,0,3:T(8,128)(2,1)} %bitcast.30, bf16[3,512,1536]{2,1,0:T(8,128)(2,1)} %bitcast.28, bf16[1,1024,512]{2,1,0:T(8,128)(2,1)S(1)} %copy-done), kind=kOutput, calls=%fused_computation | convolution fusion | flops 4838391808 | bytes 8388608 | tf_op jit(solution)/shard_map/dot_general | solution.py:47
  54.2 0.2 multiply_reduce_fusion.1
  54.4 0.5 exponential_reduce_fusion
  54.9 15.2 %pmax.7 = f32[512]{0:T(512)S(1)} all-reduce(f32[512]{0:T(512)S(1)} %multiply_reduce_fusion.1), channel_id=1, replica_groups=mesh['tm'=4,'tmpl'=8] {'tmpl'}, use_global_device_ids=true, to_apply=%region_4.5 | all-reduce | flops 512 | bytes 4096 | tf_op jit(solution)/shard_map/pmax | solution.py:54
  70.1 13.6 %psum.7 = f32[512]{0:T(512)S(1)} all-reduce(f32[512]{0:T(512)S(1)} %exponential_multiply_fusion), channel_id=1, replica_groups=mesh['tm'=4,'tmpl'=8] {'tmpl'}, use_global_device_ids=true, to_apply=%region_6.7 | all-reduce | flops 512 | bytes 4096 | tf_op jit(solution)/shard_map/psum | solution.py:55
  83.7 0.6 add_add_fusion
  (5 shorter events, 0.1 us)
Async XLA Ops:
  0.0 46.7 %copy-start = (bf16[1,1024,512]{2,1,0:T(8,128)(2,1)S(1)}, bf16[1,1024,512]{2,1,0:T(8,128)(2,1)}, u32[]{:S(2)}) copy-start(bf16[1,1024,512]{2,1,0:T(8,128)(2,1)} %param.6) | copy-start | bytes 3145732
  1.8 6.1 %collective-permute-start = (bf16[3,512]{1,0:T(4,128)(2,1)S(1)}, bf16[3,512]{1,0:T(4,128)(2,1)S(1)}, u32[]{:S(2)}, u32[]{:S(2)}) collective-permute-start(bf16[3,512]{1,0:T(4,128)(2,1)S(1)} %multiply_convert_fusion), channel_id=1, source_target_pairs={{0,8},{8,16},{16,24},{1,9},{9,17},{17,25},{2,10},{10,18},{18,26},{... | collective-permute-start | bytes 9224 | tf_op jit(solution)/shard_map/ppermute | solution.py:12
  7.9 8.9 %collective-permute-start.1 = (bf16[3,512]{1,0:T(4,128)(2,1)S(1)}, bf16[3,512]{1,0:T(4,128)(2,1)S(1)}, u32[]{:S(2)}, u32[]{:S(2)}) collective-permute-start(bf16[3,512]{1,0:T(4,128)(2,1)S(1)} %collective-permute-done), channel_id=1, source_target_pairs={{0,8},{8,16},{16,24},{1,9},{9,17},{17,25},{2,10},{10,18},{18,26},{... | collective-permute-start | bytes 9224 | tf_op jit(solution)/shard_map/ppermute | solution.py:12
  40.5 2.8 %slice-start = ((bf16[3,787455]{1,0:T(4,128)(2,1)}), bf16[3,786432]{1,0:T(4,128)(2,1)S(1)}, s32[]{:S(2)}) async-start(bf16[3,787455]{1,0:T(4,128)(2,1)} %tile.10), calls=%async_computation | async-start | bytes 12582912 | tf_op jit(solution)/shard_map/slice | solution.py:25
where the time goes:
time: 84.6 us; the launch traced here: 84.3 us
  local copies, waits for them, and re-layouts  35.3 us (42%)
  blocking collectives  28.8 us (34%)
  starting transfers between devices  9 us (11%)
  matrix products  7.46 us (9%)
  other arithmetic  2.36 us (3%)
  waiting for transfers between devices  1.31 us (2%)
    unnamed x5, local copies, waits for them, and re-layouts  18.8 us
    pmax x1, blocking collectives, shards(): overall = lax.pmax(local_peak, 'tmpl')  15.2 us
    psum x1, blocking collectives, shards(): total = lax.psum(local_total * jnp.exp(local_peak - overall), 'tmpl')  13.6 us
    another operation x2, local copies, waits for them, and re-layouts, sliding_windows(): repeated = jnp.tile(extended, (1, segment_length + 1))  10.4 us
    ppermute x2, starting transfers between devices, shifted(): return lax.ppermute(block, axis, route)  9 us
    dot_general x1, matrix products, shards(): jnp.dot(flat, mixing.reshape(basis_width, 2 * template_count), preferred_...  7.46 us
    slice x2, local copies, waits for them, and re-layouts, sliding_windows(): repeated[:, :segment_length * (span + 1)]  2.78 us
    dot_general x1, local copies, waits for them, and re-layouts, shards(): jnp.dot(flat, mixing.reshape(basis_width, 2 * template_count), preferred_...  2.52 us
  transfers between devices with their start and end apart: 2, of which 1 were waited for; matrix products, arithmetic and copies ran while one was open for 6% of the time, Pallas kernels for 0%

commit v1 on v0

v1 whole, which is shorter than its diff:
```python
import functools
import math

import jax
import jax.numpy as jnp
from jax import lax
from jax.experimental import pallas as pl
from jax.experimental.pallas import tpu as pltpu
from jax.sharding import PartitionSpec as P

MESH = pl.DeviceIdType.MESH
LANES = 128
ROWS = 8


def kernel(
    tm_count,
    tmpl_count,
    strain_ref,
    gates_ref,
    filters_hbm,
    mixing_hbm,
    out_ref,
    filters_ref,
    mixing_ref,
    ext_ref,
    hankel_ref,
    basis_ref,
    score_ref,
    gather_ref,
    load_sems,
    halo_send,
    halo_recv,
    out_send,
    out_recv,
):
    dets, seg = strain_ref.shape
    taps, width = filters_ref.shape
    templates = mixing_ref.shape[2]
    hops = (taps + seg - 2) // seg
    tm = lax.axis_index("tm")
    tmpl = lax.axis_index("tmpl")

    loads = [
        pltpu.make_async_copy(filters_hbm.at[0], filters_ref, load_sems.at[0]),
        pltpu.make_async_copy(mixing_hbm, mixing_ref, load_sems.at[1]),
    ]
    for load in loads:
        load.start()

    barrier = pltpu.get_barrier_semaphore()
    reach = sorted({o % tm_count for h in range(1, hops + 1) for o in (h, -h)} - {0})
    for o in reach:
        pl.semaphore_signal(
            barrier, inc=1, device_id=(lax.rem(tm + o, tm_count), tmpl), device_id_type=MESH
        )
    for o in range(1, tmpl_count):
        pl.semaphore_signal(
            barrier, inc=1, device_id=(tm, lax.rem(tmpl + o, tmpl_count)), device_id_type=MESH
        )

    positions = tm * seg + lax.broadcasted_iota(jnp.int32, (1, seg), 1)
    passed = jnp.zeros((1, seg), jnp.int32)
    bound = jnp.int32(0)
    for g in range(gates_ref.shape[0]):
        bound = bound + gates_ref[g]
        passed = passed + (bound <= positions).astype(jnp.int32)
    keep = ((passed & 1) == 0).astype(jnp.float32)
    ext_ref[hops] = (strain_ref[...] * keep).astype(jnp.bfloat16).astype(jnp.float32)

    pl.semaphore_wait(barrier, len(reach) + tmpl_count - 1)
    halos = []
    for h in range(1, hops + 1):
        halo = pltpu.make_async_remote_copy(
            src_ref=ext_ref.at[hops],
            dst_ref=ext_ref.at[hops - h],
            send_sem=halo_send.at[h - 1],
            recv_sem=halo_recv.at[h - 1],
            device_id=(lax.rem(tm + h, tm_count), tmpl),
            device_id_type=MESH,
        )
        halo.start()
        halos.append(halo)

    per_piece = seg // LANES
    blocks = (hops + 1) * per_piece
    row = lax.broadcasted_iota(jnp.int32, (ROWS, LANES), 0)
    lane = lax.broadcasted_iota(jnp.int32, (ROWS, LANES), 1)
    inside = [lane + row + (r + 1) < LANES for r in range(0, LANES, ROWS)]

    def skewed(d, m):
        piece = m // per_piece
        at = (m % per_piece) * LANES
        line = ext_ref[piece, d : d + 1, at : at + LANES]
        if piece < hops:
            line = jnp.where(tm >= hops - piece, line, 0.0)
        wide = jnp.broadcast_to(line, (ROWS, LANES))
        tilted = pltpu.roll(wide, LANES - 1, 1)
        for bit in (1, 2, 4):
            tilted = jnp.where((row & bit) == 0, tilted, pltpu.roll(tilted, LANES - bit, 1))
        return [tilted if r == 0 else pltpu.roll(tilted, LANES - r, 1) for r in range(0, LANES, ROWS)]

    def fill(d, first, last):
        now = skewed(d, first)
        for m in range(first, last):
            later = skewed(d, m + 1)
            tiles = [jnp.where(i, a, b) for i, a, b in zip(inside, now, later)]
            hankel_ref[d, m * LANES : (m + 1) * LANES, :] = jnp.concatenate(tiles, axis=0).astype(
                jnp.bfloat16
            )
            now = later

    own = hops * per_piece
    for d in range(dets):
        fill(d, own, blocks - 1)
    for load in loads:
        load.wait()
    for halo in halos:
        halo.wait()
    for d in range(dets):
        fill(d, 0, own)
        windows = jnp.concatenate(
            [hankel_ref[d, k : k + seg, :] for k in range(0, taps, LANES)], axis=1
        )
        basis = jnp.dot(windows, filters_ref[...], preferred_element_type=jnp.float32)
        basis_ref[d] = basis.astype(jnp.bfloat16)

    step = 256
    for j in range(0, templates, step):
        total = None
        for d in range(dets):
            for c in range(2):
                signal = jnp.dot(
                    basis_ref[d],
                    mixing_ref[c, :, j : j + step],
                    preferred_element_type=jnp.float32,
                )
                total = signal * signal if total is None else total + signal * signal
        score_ref[:, j : j + step] = 0.5 * total

    for t in range(0, seg, LANES):
        tiles = [score_ref[t : t + LANES, j : j + LANES] for j in range(0, templates, LANES)]
        peak = functools.reduce(jnp.maximum, tiles)
        mass = functools.reduce(jnp.add, [jnp.exp(tile - peak) for tile in tiles])
        peak, mass = peak.T, mass.T
        top = jnp.max(peak, axis=0, keepdims=True)
        mass = jnp.sum(mass * jnp.exp(peak - top), axis=0, keepdims=True)
        gather_ref[tmpl, :, t : t + LANES] = top + jnp.log(mass)

    sends = []
    for o in range(1, tmpl_count):
        send = pltpu.make_async_remote_copy(
            src_ref=gather_ref.at[tmpl],
            dst_ref=gather_ref.at[tmpl],
            send_sem=out_send.at[o],
            recv_sem=out_recv.at[o],
            device_id=(tm, lax.rem(tmpl + o, tmpl_count)),
            device_id_type=MESH,
        )
        send.start()
        sends.append(send)
    for send in sends:
        send.wait()
    parts = [gather_ref[i] for i in range(tmpl_count)]
    top = functools.reduce(jnp.maximum, parts)
    mass = functools.reduce(jnp.add, [jnp.exp(part - top) for part in parts])
    out_ref[...] = top + jnp.log(mass) - math.log(templates * tmpl_count)


def shards(tm_count, tmpl_count, strain, gate_lengths, filters, mixing):
    dets, seg = strain.shape
    _, taps, width = filters.shape
    templates = mixing.shape[2]
    hops = (taps + seg - 2) // seg
    mixing = mixing.transpose(1, 0, 2)
    out = pl.pallas_call(
        functools.partial(kernel, tm_count, tmpl_count),
        out_shape=jax.ShapeDtypeStruct((1, seg), jnp.float32),
        in_specs=[
            pl.BlockSpec(memory_space=pltpu.VMEM),
            pl.BlockSpec(memory_space=pltpu.SMEM),
            pl.BlockSpec(memory_space=pl.ANY),
            pl.BlockSpec(memory_space=pl.ANY),
        ],
        out_specs=pl.BlockSpec(memory_space=pltpu.VMEM),
        scratch_shapes=[
            pltpu.VMEM((taps, width), jnp.bfloat16),
            pltpu.VMEM((2, width, templates), jnp.bfloat16),
            pltpu.VMEM((hops + 1, dets, seg), jnp.float32),
            pltpu.VMEM((dets, hops * seg + seg - LANES, LANES), jnp.bfloat16),
            pltpu.VMEM((dets, seg, width), jnp.bfloat16),
            pltpu.VMEM((seg, templates), jnp.float32),
            pltpu.VMEM((tmpl_count, 1, seg), jnp.float32),
            pltpu.SemaphoreType.DMA((2,)),
            pltpu.SemaphoreType.DMA((hops,)),
            pltpu.SemaphoreType.DMA((hops,)),
            pltpu.SemaphoreType.DMA((tmpl_count,)),
            pltpu.SemaphoreType.DMA((tmpl_count,)),
        ],
        compiler_params=pltpu.CompilerParams(
            collective_id=0, has_side_effects=True, vmem_limit_bytes=40 * 2**20
        ),
    )(strain, gate_lengths, filters, mixing)
    return out.reshape(seg)


def solution(mesh):
    body = functools.partial(shards, mesh.shape["tm"], mesh.shape["tmpl"])
    in_specs = (P(None, "tm"), P(), P("tmpl", None, None), P(None, None, "tmpl"))
    return jax.shard_map(body, mesh=mesh, in_specs=in_specs, out_specs=P("tm"), check_vma=False)
```

time: 84.6 us -> 22.4 us (0.26)
  local copies, waits for them, and re-layouts: 35.3 us -> 2.88 us
  blocking collectives: 28.8 us -> 0 us
  Pallas kernels: 0 us -> 19.3 us
  starting transfers between devices: 9 us -> 0 us
  matrix products: 7.46 us -> 0 us
  other arithmetic: 2.36 us -> 0 us
  waiting for transfers between devices: 1.31 us -> 0 us
    pallas_call x0 -> x1, Pallas kernels: none -> 19.3 us  [shards(): pl.pallas_call(functools.partial(kernel, tm_count, tmpl_count), out_shape...]
    unnamed x5 -> x8, local copies, waits for them, and re-layouts: 18.8 us -> 2.88 us
    pmax x1 -> x0, blocking collectives: 15.2 us -> none  [shards(): overall = lax.pmax(local_peak, 'tmpl')]
    psum x1 -> x0, blocking collectives: 13.6 us -> none  [shards(): total = lax.psum(local_total * jnp.exp(local_peak - overall), 'tmpl')]
    another operation x3 -> x0, local copies, waits for them, and re-layouts: 11.2 us -> none  [the longest x2 10.4 us: sliding_windows(): repeated = jnp.tile(extended, (1, segment_length + 1))]
    ppermute x2 -> x0, starting transfers between devices: 9 us -> none  [shifted(): return lax.ppermute(block, axis, route)]
    dot_general x1 -> x0, matrix products: 7.46 us -> none  [shards(): jnp.dot(flat, mixing.reshape(basis_width, 2 * template_count), preferred_...]
    slice x2 -> x0, local copies, waits for them, and re-layouts: 2.78 us -> none  [sliding_windows(): repeated[:, :segment_length * (span + 1)]]
  transfers between devices with their start and end apart: 2 -> 0, of which waited for: 1 -> 0; matrix products, arithmetic and copies ran while one was open for 6% -> 0% of each run, Pallas kernels for 0% -> 0%
where the time goes in v1:
time: 22.4 us; the launch traced here: 22.2 us
  Pallas kernels  19.3 us (86%)
  local copies, waits for them, and re-layouts  2.88 us (13%)
    pallas_call x1, Pallas kernels, shards(): pl.pallas_call(functools.partial(kernel, tm_count, tmpl_count), out_shape...  19.3 us
    unnamed x8, local copies, waits for them, and re-layouts  2.88 us

profile of v1, /device:TPU:0, one launch (start us, length us, event | category | flops | bytes accessed | tf_op | source)
XLA Modules:
  0.0 22.2 jit_solution(11830517424602016920)
XLA Ops:
  0.0 0.0 copy-start
  0.0 0.0 copy-start.2
  0.0 0.0 copy-start.1
  0.0 2.3 %copy.7 = bf16[512,2,1024]{2,0,1:T(8,128)(2,1)S(1)} copy(bf16[512,2,1024]{2,1,0:T(2,128)(2,1)} %param.7) | data formatting | bytes 4194304 | tf_op args[3]
  2.3 0.0 copy-done
  2.3 0.0 copy-done.2
  2.3 0.0 copy-done.1
  2.3 19.3 %shard_map.46 = f32[1,512]{1,0:T(1,128)S(1)} custom-call(f32[3,512]{1,0:T(4,128)S(1)} %copy-done.1, s32[16]{0:T(128)S(1)} %copy-done.2, bf16[1,1024,512]{2,1,0:T(8,128)(2,1)S(1)} %copy-done, bf16[2,512,1024]{2,1,0:T(8,128)(2,1)S(1)} %bitcast.4), custom_call_target="tpu_custom_call" | custom-call | tf_op jit(solution)/shard_map/pallas_call | solution.py:176
  21.6 0.6 %copy.9 = f32[512]{0:T(512)} copy(f32[512]{0:T(512)S(1)} %bitcast.5) | data formatting | bytes 4096
Async XLA Ops:
  0.0 2.3 %copy-start = (bf16[1,1024,512]{2,1,0:T(8,128)(2,1)S(1)}, bf16[1,1024,512]{2,1,0:T(8,128)(2,1)}, u32[]{:S(2)}) copy-start(bf16[1,1024,512]{2,1,0:T(8,128)(2,1)} %filters_hbm.1) | copy-start | bytes 3145732
  0.0 2.3 %copy-start.2 = (s32[16]{0:T(128)S(1)}, s32[16]{0:T(128)}, u32[]{:S(2)}) copy-start(s32[16]{0:T(128)} %gates_ref.1) | copy-start | bytes 196
  0.0 2.3 %copy-start.1 = (f32[3,512]{1,0:T(4,128)S(1)}, f32[3,512]{1,0:T(4,128)}, u32[]{:S(2)}) copy-start(f32[3,512]{1,0:T(4,128)} %strain_ref.1) | copy-start | bytes 18436

commit v2 on v1

--- a/solution.py
+++ b/solution.py
@@ -11,17 +11,21 @@
 MESH = pl.DeviceIdType.MESH
 LANES = 128
 ROWS = 8
+CHUNKS = 4
 
 
 def kernel(
     tm_count,
     tmpl_count,
-    strain_ref,
-    gates_ref,
+    strain_hbm,
+    gates_hbm,
     filters_hbm,
     mixing_hbm,
     out_ref,
+    strain_ref,
+    gates_ref,
     filters_ref,
+    raw_ref,
     mixing_ref,
     ext_ref,
     hankel_ref,
@@ -41,13 +45,6 @@
     tm = lax.axis_index("tm")
     tmpl = lax.axis_index("tmpl")
 
-    loads = [
-        pltpu.make_async_copy(filters_hbm.at[0], filters_ref, load_sems.at[0]),
-        pltpu.make_async_copy(mixing_hbm, mixing_ref, load_sems.at[1]),
-    ]
-    for load in loads:
-        load.start()
-
     barrier = pltpu.get_barrier_semaphore()
     reach = sorted({o % tm_count for h in range(1, hops + 1) for o in (h, -h)} - {0})
     for o in reach:
@@ -58,6 +55,25 @@
         pl.semaphore_signal(
             barrier, inc=1, device_id=(tm, lax.rem(tmpl + o, tmpl_count)), device_id_type=MESH
         )
+
+    small = [
+        pltpu.make_async_copy(strain_hbm, strain_ref, load_sems.at[0]),
+        pltpu.make_async_copy(gates_hbm, gates_ref, load_sems.at[1]),
+    ]
+    chunk = width // CHUNKS
+    mixing_loads = [
+        pltpu.make_async_copy(
+            mixing_hbm.at[pl.ds(i * chunk, chunk)],
+            raw_ref.at[pl.ds(i * chunk, chunk)],
+            load_sems.at[3 + i],
+        )
+        for i in range(CHUNKS)
+    ]
+    filters_load = pltpu.make_async_copy(filters_hbm.at[0], filters_ref, load_sems.at[2])
+    for load in small + mixing_loads + [filters_load]:
+        load.start()
+    for load in small:
+        load.wait()
 
     positions = tm * seg + lax.broadcasted_iota(jnp.int32, (1, seg), 1)
     passed = jnp.zeros((1, seg), jnp.int32)
@@ -86,7 +102,7 @@
     blocks = (hops + 1) * per_piece
     row = lax.broadcasted_iota(jnp.int32, (ROWS, LANES), 0)
     lane = lax.broadcasted_iota(jnp.int32, (ROWS, LANES), 1)
-    inside = [lane + row + (r + 1) < LANES for r in range(0, LANES, ROWS)]
+    inside = [lane - row + (r + ROWS) < LANES for r in range(0, LANES, ROWS)]
 
     def skewed(d, m):
         piece = m // per_piece
@@ -95,10 +111,10 @@
         if piece < hops:
             line = jnp.where(tm >= hops - piece, line, 0.0)
         wide = jnp.broadcast_to(line, (ROWS, LANES))
-        tilted = pltpu.roll(wide, LANES - 1, 1)
-        for bit in (1, 2, 4):
-            tilted = jnp.where((row & bit) == 0, tilted, pltpu.roll(tilted, LANES - bit, 1))
-        return [tilted if r == 0 else pltpu.roll(tilted, LANES - r, 1) for r in range(0, LANES, ROWS)]
+        return [
+            pltpu.roll(wide, LANES - ROWS - r, 1, stride=1, stride_axis=0)
+            for r in range(0, LANES, ROWS)
+        ]
 
     def fill(d, first, last):
         now = skewed(d, first)
@@ -113,8 +129,12 @@
     own = hops * per_piece
     for d in range(dets):
         fill(d, own, blocks - 1)
-    for load in loads:
+    for i, load in enumerate(mixing_loads):
         load.wait()
+        part = jnp.swapaxes(raw_ref[i * chunk : (i + 1) * chunk], 0, 1)
+        for c in range(2):
+            mixing_ref[c, i * chunk : (i + 1) * chunk, :] = part[c]
+    filters_load.wait()
     for halo in halos:
         halo.wait()
     for d in range(dets):
@@ -138,6 +158,7 @@
                 total = signal * signal if total is None else total + signal * signal
         score_ref[:, j : j + step] = 0.5 * total
 
+    lanes = lax.broadcasted_iota(jnp.int32, (1, LANES), 1)
     for t in range(0, seg, LANES):
         tiles = [score_ref[t : t + LANES, j : j + LANES] for j in range(0, templates, LANES)]
         peak = functools.reduce(jnp.maximum, tiles)
@@ -145,7 +166,12 @@
         peak, mass = peak.T, mass.T
         top = jnp.max(peak, axis=0, keepdims=True)
         mass = jnp.sum(mass * jnp.exp(peak - top), axis=0, keepdims=True)
-        gather_ref[tmpl, :, t : t + LANES] = top + jnp.log(mass)
+        line = top + jnp.log(mass)
+        for bit in (1, 2, 4):
+            line = jnp.where(
+                (lanes & bit) == 0, pltpu.roll(line, LANES - bit, 1), pltpu.roll(line, bit, 1)
+            )
+        gather_ref[tmpl, :, t : t + LANES] = line
 
     sends = []
     for o in range(1, tmpl_count):
@@ -172,33 +198,30 @@
     _, taps, width = filters.shape
     templates = mixing.shape[2]
     hops = (taps + seg - 2) // seg
-    mixing = mixing.transpose(1, 0, 2)
     out = pl.pallas_call(
         functools.partial(kernel, tm_count, tmpl_count),
         out_shape=jax.ShapeDtypeStruct((1, seg), jnp.float32),
-        in_specs=[
-            pl.BlockSpec(memory_space=pltpu.VMEM),
-            pl.BlockSpec(memory_space=pltpu.SMEM),
-            pl.BlockSpec(memory_space=pl.ANY),
-            pl.BlockSpec(memory_space=pl.ANY),
-        ],
+        in_specs=[pl.BlockSpec(memory_space=pltpu.HBM)] * 4,
         out_specs=pl.BlockSpec(memory_space=pltpu.VMEM),
         scratch_shapes=[
+            pltpu.VMEM((dets, seg), jnp.float32),
+            pltpu.SMEM(gate_lengths.shape, jnp.int32),
             pltpu.VMEM((taps, width), jnp.bfloat16),
+            pltpu.VMEM((width, 2, templates), jnp.bfloat16),
             pltpu.VMEM((2, width, templates), jnp.bfloat16),
             pltpu.VMEM((hops + 1, dets, seg), jnp.float32),
             pltpu.VMEM((dets, hops * seg + seg - LANES, LANES), jnp.bfloat16),
             pltpu.VMEM((dets, seg, width), jnp.bfloat16),
             pltpu.VMEM((seg, templates), jnp.float32),
             pltpu.VMEM((tmpl_count, 1, seg), jnp.float32),
-            pltpu.SemaphoreType.DMA((2,)),
+            pltpu.SemaphoreType.DMA((3 + CHUNKS,)),
             pltpu.SemaphoreType.DMA((hops,)),
             pltpu.SemaphoreType.DMA((hops,)),
             pltpu.SemaphoreType.DMA((tmpl_count,)),
             pltpu.SemaphoreType.DMA((tmpl_count,)),
         ],
         compiler_params=pltpu.CompilerParams(
-            collective_id=0, has_side_effects=True, vmem_limit_bytes=40 * 2**20
+            collective_id=0, has_side_effects=True, vmem_limit_bytes=60 * 2**20
         ),
     )(strain, gate_lengths, filters, mixing)
     return out.reshape(seg)

time: 22.4 us -> 19.7 us (0.88)
  local copies, waits for them, and re-layouts: 2.88 us -> 1.26 us
  Pallas kernels: 19.3 us -> 18.2 us
    unnamed x8 -> x1, local copies, waits for them, and re-layouts: 2.88 us -> 1.26 us
    pallas_call x1, Pallas kernels: 19.3 us -> 18.2 us  [shards(): pl.pallas_call(functools.partial(kernel, tm_count, tmpl_count), out_shape...]
where the time goes in v2:
time: 19.7 us; the launch traced here: 19.5 us
  Pallas kernels  18.2 us (92%)
  local copies, waits for them, and re-layouts  1.26 us (6%)
    pallas_call x1, Pallas kernels, shards(): pl.pallas_call(functools.partial(kernel, tm_count, tmpl_count), out_shape...  18.2 us
    unnamed x1, local copies, waits for them, and re-layouts  1.26 us

profile of v2, /device:TPU:0, one launch (start us, length us, event | category | flops | bytes accessed | tf_op | source)
XLA Modules:
  0.0 19.5 jit_solution(4107908052809225313)
XLA Ops:
  0.0 18.2 %shard_map.46 = f32[1,512]{1,0:T(1,128)} custom-call(f32[3,512]{1,0:T(4,128)} %strain_hbm.1, s32[16]{0:T(128)} %gates_hbm.1, bf16[1,1024,512]{2,1,0:T(8,128)(2,1)} %filters_hbm.1, bf16[512,2,1024]{2,1,0:T(2,128)(2,1)} %mixing_hbm.1), custom_call_target="tpu_custom_call" | custom-call | tf_op jit(solution)/shard_map/pallas_call | solution.py:201
  18.2 1.3 %copy.6 = f32[512]{0:T(512)} copy(f32[512]{0:T(512)} %bitcast.1) | data formatting | bytes 4096

commit v3 on v2

--- a/solution.py
+++ b/solution.py
@@ -37,6 +37,7 @@
     halo_recv,
     out_send,
     out_recv,
+    ready_sems,
 ):
     dets, seg = strain_ref.shape
     taps, width = filters_ref.shape
@@ -51,10 +52,28 @@
         pl.semaphore_signal(
             barrier, inc=1, device_id=(lax.rem(tm + o, tm_count), tmpl), device_id_type=MESH
         )
-    for o in range(1, tmpl_count):
-        pl.semaphore_signal(
-            barrier, inc=1, device_id=(tm, lax.rem(tmpl + o, tmpl_count)), device_id_type=MESH
-        )
+    cores = 2
+    chips = tmpl_count // cores
+    chip, core = tmpl // cores, lax.rem(tmpl, cores)
+    pl.semaphore_signal(barrier, inc=1, device_id=(tm, chip * cores + 1 - core), device_id_type=MESH)
+
+    def tell(sem, distance):
+        @pl.when(chip + distance < chips)
+        def _():
+            pl.semaphore_signal(
+                sem, inc=1, device_id=(tm, tmpl + distance * cores), device_id_type=MESH
+            )
+
+        @pl.when(chip >= distance)
+        def _():
+            pl.semaphore_signal(
+                sem, inc=1, device_id=(tm, tmpl - distance * cores), device_id_type=MESH
+            )
+
+    def told(distance):
+        return (chip + distance < chips).astype(jnp.int32) + (chip >= distance).astype(jnp.int32)
+
+    tell(barrier, 1)
 
     small = [
         pltpu.make_async_copy(strain_hbm, strain_ref, load_sems.at[0]),
@@ -84,7 +103,7 @@
     keep = ((passed & 1) == 0).astype(jnp.float32)
     ext_ref[hops] = (strain_ref[...] * keep).astype(jnp.bfloat16).astype(jnp.float32)
 
-    pl.semaphore_wait(barrier, len(reach) + tmpl_count - 1)
+    pl.semaphore_wait(barrier, len(reach) + 1 + told(1))
     halos = []
     for h in range(1, hops + 1):
         halo = pltpu.make_async_remote_copy(
@@ -97,6 +116,7 @@
         )
         halo.start()
         halos.append(halo)
+    tell(ready_sems.at[0], 1)
 
     per_piece = seg // LANES
     blocks = (hops + 1) * per_piece
@@ -137,6 +157,10 @@
     filters_load.wait()
     for halo in halos:
         halo.wait()
+    pl.semaphore_wait(ready_sems.at[0], told(1))
+    distance = 2
+    if distance < chips:
+        tell(ready_sems.at[1], distance)
     for d in range(dets):
         fill(d, 0, own)
         windows = jnp.concatenate(
@@ -173,6 +197,12 @@
             )
         gather_ref[tmpl, :, t : t + LANES] = line
 
+    level = 1
+    while distance < chips:
+        pl.semaphore_wait(ready_sems.at[level], told(distance))
+        distance, level = 2 * distance, level + 1
+        if distance < chips:
+            tell(ready_sems.at[level], distance)
     sends = []
     for o in range(1, tmpl_count):
         send = pltpu.make_async_remote_copy(
@@ -190,7 +220,7 @@
     parts = [gather_ref[i] for i in range(tmpl_count)]
     top = functools.reduce(jnp.maximum, parts)
     mass = functools.reduce(jnp.add, [jnp.exp(part - top) for part in parts])
-    out_ref[...] = top + jnp.log(mass) - math.log(templates * tmpl_count)
+    out_ref[...] = top + jnp.log(mass)
 
 
 def shards(tm_count, tmpl_count, strain, gate_lengths, filters, mixing):
@@ -219,12 +249,13 @@
             pltpu.SemaphoreType.DMA((hops,)),
             pltpu.SemaphoreType.DMA((tmpl_count,)),
             pltpu.SemaphoreType.DMA((tmpl_count,)),
+            pltpu.SemaphoreType.REGULAR((max(2, tmpl_count.bit_length()),)),
         ],
         compiler_params=pltpu.CompilerParams(
             collective_id=0, has_side_effects=True, vmem_limit_bytes=60 * 2**20
         ),
     )(strain, gate_lengths, filters, mixing)
-    return out.reshape(seg)
+    return out.reshape(seg) - math.log(templates * tmpl_count)
 
 
 def solution(mesh):

time: 19.7 us -> 19.7 us (level)
  other arithmetic: 0 us -> 1.26 us
  local copies, waits for them, and re-layouts: 1.26 us -> 0 us
    sub x0 -> x1, other arithmetic: none -> 1.26 us  [shards(): return out.reshape(seg) - math.log(templates * tmpl_count)]
    unnamed x1 -> x0, local copies, waits for them, and re-layouts: 1.26 us -> none
where the time goes in v3:
time: 19.7 us; the launch traced here: 19.5 us
  Pallas kernels  18.2 us (92%)
  other arithmetic  1.26 us (6%)
    pallas_call x1, Pallas kernels, shards(): pl.pallas_call(functools.partial(kernel, tm_count, tmpl_count), out_shape...  18.2 us
    sub x1, other arithmetic, shards(): return out.reshape(seg) - math.log(templates * tmpl_count)  1.26 us

profile of v3, /device:TPU:0, one launch (start us, length us, event | category | flops | bytes accessed | tf_op | source)
XLA Modules:
  0.0 19.5 jit_solution(2119568021432796155)
XLA Ops:
  0.0 18.2 %shard_map.46 = f32[1,512]{1,0:T(1,128)} custom-call(f32[3,512]{1,0:T(4,128)} %strain_hbm.1, s32[16]{0:T(128)} %gates_hbm.1, bf16[1,1024,512]{2,1,0:T(8,128)(2,1)} %filters_hbm.1, bf16[512,2,1024]{2,1,0:T(2,128)(2,1)} %mixing_hbm.1), custom_call_target="tpu_custom_call" | custom-call | tf_op jit(solution)/shard_map/pallas_call | solution.py:231
  18.2 1.3 %broadcast_add_fusion = f32[1,512]{1,0:T(1,128)} fusion(f32[1,512]{1,0:T(1,128)} %shard_map.46), kind=kLoop, calls=%fused_computation | loop fusion | flops 512 | bytes 4096 | tf_op jit(solution)/shard_map/sub | solution.py:258

commit v4 on v3

--- a/solution.py
+++ b/solution.py
@@ -47,11 +47,14 @@
     tmpl = lax.axis_index("tmpl")
 
     barrier = pltpu.get_barrier_semaphore()
-    reach = sorted({o % tm_count for h in range(1, hops + 1) for o in (h, -h)} - {0})
-    for o in reach:
-        pl.semaphore_signal(
-            barrier, inc=1, device_id=(lax.rem(tm + o, tm_count), tmpl), device_id_type=MESH
-        )
+    for h in range(1, hops + 1):
+
+        @pl.when(tm >= h)
+        def _():
+            pl.semaphore_signal(barrier, inc=1, device_id=(tm - h, tmpl), device_id_type=MESH)
+
+    receivers = sum((tm + h < tm_count).astype(jnp.int32) for h in range(1, hops + 1))
+
     cores = 2
     chips = tmpl_count // cores
     chip, core = tmpl // cores, lax.rem(tmpl, cores)
@@ -103,7 +106,7 @@
     keep = ((passed & 1) == 0).astype(jnp.float32)
     ext_ref[hops] = (strain_ref[...] * keep).astype(jnp.bfloat16).astype(jnp.float32)
 
-    pl.semaphore_wait(barrier, len(reach) + 1 + told(1))
+    pl.semaphore_wait(barrier, receivers + 1 + told(1))
     halos = []
     for h in range(1, hops + 1):
         halo = pltpu.make_async_remote_copy(
@@ -111,11 +114,16 @@
             dst_ref=ext_ref.at[hops - h],
             send_sem=halo_send.at[h - 1],
             recv_sem=halo_recv.at[h - 1],
-            device_id=(lax.rem(tm + h, tm_count), tmpl),
+            device_id=(tm + h, tmpl),
             device_id_type=MESH,
         )
-        halo.start()
+        pl.when(tm + h < tm_count)(halo.start)
         halos.append(halo)
+
+        @pl.when(tm < h)
+        def _():
+            ext_ref[hops - h] = jnp.zeros((dets, seg), jnp.float32)
+
     tell(ready_sems.at[0], 1)
 
     per_piece = seg // LANES
@@ -128,8 +136,6 @@
         piece = m // per_piece
         at = (m % per_piece) * LANES
         line = ext_ref[piece, d : d + 1, at : at + LANES]
-        if piece < hops:
-            line = jnp.where(tm >= hops - piece, line, 0.0)
         wide = jnp.broadcast_to(line, (ROWS, LANES))
         return [
             pltpu.roll(wide, LANES - ROWS - r, 1, stride=1, stride_axis=0)
@@ -155,8 +161,9 @@
         for c in range(2):
             mixing_ref[c, i * chunk : (i + 1) * chunk, :] = part[c]
     filters_load.wait()
-    for halo in halos:
-        halo.wait()
+    for h, halo in enumerate(halos, 1):
+        pl.when(tm + h < tm_count)(halo.wait_send)
+        pl.when(tm >= h)(halo.wait_recv)
     pl.semaphore_wait(ready_sems.at[0], told(1))
     distance = 2
     if distance < chips:

time: 19.7 us -> 18.2 us (0.924)
  the two profiles are of different devices: /device:TPU:0 before, /device:TPU:5 now
where the time goes in v4:
time: 18.2 us; the launch traced here: 18 us
  Pallas kernels  16.7 us (92%)
  other arithmetic  1.26 us (7%)
    pallas_call x1, Pallas kernels, shards(): pl.pallas_call(functools.partial(kernel, tm_count, tmpl_count), out_shape...  16.7 us
    sub x1, other arithmetic, shards(): return out.reshape(seg) - math.log(templates * tmpl_count)  1.26 us

profile of v4, /device:TPU:5, one launch (start us, length us, event | category | flops | bytes accessed | tf_op | source)
XLA Modules:
  0.0 18.0 jit_solution(1525259192557524760)
XLA Ops:
  0.0 16.7 %shard_map.46 = f32[1,512]{1,0:T(1,128)} custom-call(f32[3,512]{1,0:T(4,128)} %strain_hbm.1, s32[16]{0:T(128)} %gates_hbm.1, bf16[1,1024,512]{2,1,0:T(8,128)(2,1)} %filters_hbm.1, bf16[512,2,1024]{2,1,0:T(2,128)(2,1)} %mixing_hbm.1), custom_call_target="tpu_custom_call" | custom-call | tf_op jit(solution)/shard_map/pallas_call | solution.py:238
  16.7 1.3 %broadcast_add_fusion = f32[1,512]{1,0:T(1,128)} fusion(f32[1,512]{1,0:T(1,128)} %shard_map.46), kind=kLoop, calls=%fused_computation | loop fusion | flops 512 | bytes 4096 | tf_op jit(solution)/shard_map/sub | solution.py:265
